TPU v7x, 32 devices: a whole 2x2x4 slice. The times are simulated.
32 devices in a mesh: frame: 4 (over x, core), tile: 8 (over z, y).
Axes of the slice: x: 2, y: 2, z: 4, core: 2. Of those that a mesh axis runs over, the one named last changes fastest.
Arguments:
- frames: bfloat16 [4, 64, 64, 2048], P('frame', None, 'tile'), may hold values from -6 to 6
- predict_w: bfloat16 [2, 4, 3, 3, 64, 64], replicated, may hold values from -0.25 to 0.25
- predict_b: float32 [2, 4, 64], replicated, may hold values from -2 to 2
- update_w: bfloat16 [2, 4, 3, 3, 64, 64], replicated, may hold values from -0.25 to 0.25
- update_b: float32 [2, 4, 64], replicated, may hold values from -2 to 2
Outputs:
- coefficients: bfloat16 [4, 64, 64, 2048], P('frame', None, 'tile')
All inputs are finite; a program needn't handle non-finite values.
Results may differ from a plain program's by a relative error of at most 0.009.
Values may be sent and summed in bfloat16 or wider, within the bound.
A program may use at most 128 MiB of HBM per device.

v0:
```python
import jax
import jax.numpy as jnp
from jax import lax
from jax.sharding import PartitionSpec as P

LAYERS = 4


def extended_2(block, sides, width):
    for axis, dim in sides:
        count = lax.axis_size(axis)
        forward = [(i, i + 1) for i in range(count - 1)]
        backward = [(target, source) for source, target in forward]
        low = lax.ppermute(
            lax.slice_in_dim(block, block.shape[dim] - width, None, axis=dim), axis, forward
        )
        high = lax.ppermute(lax.slice_in_dim(block, 0, width, axis=dim), axis, backward)
        block = jnp.concatenate([low, block, high], axis=dim)
    return block


def partner_2(x, axis, distance):
    return lax.ppermute(x, axis, [(i, i ^ 1 << distance) for i in range(lax.axis_size(axis))])


def conv_rows(extended, kernel, bias_row):
    row_count = extended.shape[1] - 2
    width = extended.shape[2]
    channels = kernel.shape[3]
    padded = jnp.pad(extended, ((0, 0), (0, 0), (1, 1)))
    stacked = jnp.concatenate(
        [padded[:, :, shift_col : shift_col + width] for shift_col in range(3)], axis=0
    )
    summed = None
    for shift_row in range(3):
        joined = jnp.transpose(kernel[shift_row], (1, 0, 2)).reshape(kernel.shape[2], 3 * channels)
        term = jnp.einsum(
            "ok,khw->ohw",
            joined,
            stacked[:, shift_row : shift_row + row_count],
            preferred_element_type=jnp.float32,
        )
        summed = term if summed is None else summed + term
    return summed + bias_row[:, None, None]


def deep_network(field, start, count, kernels, biases):
    own_rows = field.shape[1]
    total_rows = own_rows * lax.axis_size("tile")
    extended = extended_2(field, (("tile", 1),), LAYERS)
    hidden = lax.dynamic_slice_in_dim(extended, start, count + 2 * LAYERS, 1)
    first_row = lax.axis_index("tile") * own_rows + start - LAYERS
    for layer_index in range(LAYERS):
        result = conv_rows(hidden, kernels[layer_index], biases[layer_index])
        if layer_index < LAYERS - 1:
            row_count = result.shape[1]
            row_global = first_row + layer_index + 1 + jnp.arange(row_count, dtype=jnp.int32)
            inside = (row_global >= 0) & (row_global < total_rows)
            hidden = jnp.where(inside[None, :, None], jnp.maximum(result, 0.0), 0.0).astype(
                jnp.bfloat16
            )
    return result


def local(frames, predict_w, predict_b, update_w, update_b):
    own_frame = frames[0]
    own_rows = own_frame.shape[1]
    position = lax.axis_index("frame")
    is_odd = position % 2 == 1
    is_upper = position // 2 % 2 == 1
    partner = partner_2(own_frame, "frame", 0)
    even_frame = jnp.where(is_odd, partner, own_frame)
    odd_frame = jnp.where(is_odd, own_frame, partner)
    half_rows = own_rows // 2
    half_start = position % 2 * half_rows
    odd_half = lax.dynamic_slice_in_dim(odd_frame, half_start, half_rows, 1)
    even_half = lax.dynamic_slice_in_dim(even_frame, half_start, half_rows, 1)
    high_half = (
        odd_half.astype(jnp.float32)
        - deep_network(even_frame, half_start, half_rows, predict_w[0], predict_b[0])
    ).astype(jnp.bfloat16)
    other_high = partner_2(high_half, "frame", 0)
    high_one = jnp.where(
        is_odd,
        jnp.concatenate([other_high, high_half], axis=1),
        jnp.concatenate([high_half, other_high], axis=1),
    )
    low_half = (
        even_half.astype(jnp.float32)
        + deep_network(high_one, half_start, half_rows, update_w[0], update_b[0])
    ).astype(jnp.bfloat16)
    other_lowhalf = partner_2(low_half, "frame", 0)
    low_one = jnp.where(
        is_odd,
        jnp.concatenate([other_lowhalf, low_half], axis=1),
        jnp.concatenate([low_half, other_lowhalf], axis=1),
    )
    other_low = partner_2(low_one, "frame", 1)
    low_even = jnp.where(is_upper, other_low, low_one)
    low_odd = jnp.where(is_upper, low_one, other_low)
    quarter_rows = own_rows // 4
    quarter_start = position * quarter_rows
    odd_quarter = lax.dynamic_slice_in_dim(low_odd, quarter_start, quarter_rows, 1)
    even_quarter = lax.dynamic_slice_in_dim(low_even, quarter_start, quarter_rows, 1)
    high_quarter = (
        odd_quarter.astype(jnp.float32)
        - deep_network(low_even, quarter_start, quarter_rows, predict_w[1], predict_b[1])
    ).astype(jnp.bfloat16)
    high_two = lax.all_gather(high_quarter, "frame", axis=1, tiled=True)
    low_quarter = (
        even_quarter.astype(jnp.float32)
        + deep_network(high_two, quarter_start, quarter_rows, update_w[1], update_b[1])
    ).astype(jnp.bfloat16)
    low_two = lax.all_gather(low_quarter, "frame", axis=1, tiled=True)
    chosen = jnp.where(is_odd, high_one, jnp.where(is_upper, high_two, low_two))
    return chosen[None]


def solution(mesh):
    in_specs = (P("frame", None, "tile", None), P(), P(), P(), P())
    out_specs = P("frame", None, "tile", None)
    return jax.shard_map(local, mesh=mesh, in_specs=in_specs, out_specs=out_specs, check_vma=False)
```

profile of v0, /device:TPU:0, one launch (start us, length us, event | category | flops | bytes accessed | tf_op | source)
XLA Modules:
  0.0 500.0 jit_solution(11653294741060670363)
XLA Ops:
  13.8 3.9 broadcast_select_fusion.1
  19.2 5.7 %collective-permute-start.1 = (bf16[64,4,2048]{2,0,1:T(8,128)(2,1)}, bf16[64,4,2048]{2,0,1:T(8,128)(2,1)}, u32[]{:S(2)}, u32[]{:S(2)}) collective-permute-start(bf16[64,4,2048]{2,0,1:T(8,128)(2,1)} %get-tuple-element.32), channel_id=1, source_target_pairs={{0,1},{1,2},{2,3},{3,4},{4,5},{5,6},{6,7},{8,9},{9,10},{10,11},{11... | collective-permute-start | bytes 3145736 | tf_op jit(solution)/shard_map/ppermute | solution.py:14
  34.7 35.4 %collective-permute-done.1 = bf16[64,4,2048]{2,0,1:T(8,128)(2,1)} collective-permute-done((bf16[64,4,2048]{2,0,1:T(8,128)(2,1)}, bf16[64,4,2048]{2,0,1:T(8,128)(2,1)}, u32[]{:S(2)}, u32[]{:S(2)}) %collective-permute-start.1) | collective-permute-done | bytes 1048608 | tf_op jit(solution)/shard_map/ppermute | solution.py:14
  72.5 3.8 pad_slice_fusion.3
  79.2 4.0 fusion.61
  83.1 5.3 %fusion.4 = bf16[64,10,2048]{2,0,1:T(8,128)(2,1)S(1)} fusion(bf16[64,192,1]{0,1,2:T(8,128)(2,1)S(1)} %bitcast.473, f32[10,2048,64]{1,2,0:T(8,128)} %fusion.61, f32[10,2048,64]{1,2,0:T(8,128)S(1)} %fusion.60, f32[64]{0:T(128)S(1)} %get-tuple-element.107, pred[10]{0:T(512)(128)(4,1)S(1)} %compare_and_fusion.3, ...), kind=kOutput, calls=%fused_computation.46 | convolution fusion | flops 539492352 | bytes 22569226 | tf_op jit(solution)/shard_map/ok,khw->ohw/dot_general | solution.py:37
  100.6 3.6 fusion.48
  104.3 4.0 fusion.49
  121.5 5.3 %collective-permute-start.4 = (bf16[64,4,2048]{2,0,1:T(8,128)(2,1)}, bf16[64,4,2048]{2,0,1:T(8,128)(2,1)}, u32[]{:S(2)}, u32[]{:S(2)}) collective-permute-start(bf16[64,4,2048]{2,0,1:T(8,128)(2,1)} %get-tuple-element.28), channel_id=1, source_target_pairs={{0,1},{1,2},{2,3},{3,4},{4,5},{5,6},{6,7},{8,9},{9,10},{10,11},{11... | collective-permute-start | bytes 3145736 | tf_op jit(solution)/shard_map/ppermute | solution.py:14
  136.5 34.8 %collective-permute-done.4 = bf16[64,4,2048]{2,0,1:T(8,128)(2,1)} collective-permute-done((bf16[64,4,2048]{2,0,1:T(8,128)(2,1)}, bf16[64,4,2048]{2,0,1:T(8,128)(2,1)}, u32[]{:S(2)}, u32[]{:S(2)}) %collective-permute-start.4) | collective-permute-done | bytes 1048608 | tf_op jit(solution)/shard_map/ppermute | solution.py:14
  173.9 3.8 pad_slice_fusion.1
  180.4 4.0 fusion.59
  184.4 5.3 %fusion.5 = bf16[64,10,2048]{2,0,1:T(8,128)(2,1)S(1)} fusion(bf16[64,192,1]{0,1,2:T(8,128)(2,1)S(1)} %bitcast.492, f32[10,2048,64]{1,2,0:T(8,128)} %fusion.59, f32[10,2048,64]{1,2,0:T(8,128)S(1)} %fusion.58, f32[64]{0:T(128)S(1)} %get-tuple-element.99, pred[10]{0:T(512)(128)(4,1)S(1)} %compare_and_fusion.3, bf16[64,12,2048]{2,0,1:T(8,128)(2,1)S(1)} %get-tuple-element.6, ...), kind=kOutput, calls=%fused_computation.47 | convolution fusion | flops 539492352 | bytes 22569226 | tf_op jit(solution)/shard_map/ok,khw->ohw/dot_general | solution.py:37
  201.9 3.6 fusion.46
  205.5 4.0 fusion.47
  221.5 46.3 %collective-permute-done.7 = bf16[64,8,2048]{2,0,1:T(8,128)(2,1)} collective-permute-done((bf16[64,8,2048]{2,0,1:T(8,128)(2,1)S(1)}, bf16[64,8,2048]{2,0,1:T(8,128)(2,1)}, u32[]{:S(2)}, u32[]{:S(2)}) %collective-permute-start.7) | collective-permute-done | bytes 2097184 | tf_op jit(solution)/shard_map/ppermute | solution.py:23
  271.1 4.4 collective-permute-start.8
  284.5 35.7 %collective-permute-done.8 = bf16[64,4,2048]{2,0,1:T(8,128)(2,1)S(1)} collective-permute-done((bf16[64,4,2048]{2,0,1:T(8,128)(2,1)}, bf16[64,4,2048]{2,0,1:T(8,128)(2,1)S(1)}, u32[]{:S(2)}, u32[]{:S(2)}) %collective-permute-start.8) | collective-permute-done | bytes 1048608 | tf_op jit(solution)/shard_map/ppermute | solution.py:14
  333.6 3.6 fusion.44
  337.3 3.6 fusion.45
  352.3 27.6 %all-gather.3.cloned.1.call-done = bf16[64,8,2048]{2,0,1:T(8,128)(2,1)} async-done(((bf16[64,2,2048]{2,0,1:T(8,128)(2,1)}), bf16[64,8,2048]{2,0,1:T(8,128)(2,1)}) %all-gather.3.cloned.1.call-update) | async-done | bytes 2097168 | tf_op jit(solution)/shard_map/all_gather | solution.py:109
  395.3 36.7 %collective-permute-done.10 = bf16[64,4,2048]{2,0,1:T(8,128)(2,1)S(1)} collective-permute-done((bf16[64,4,2048]{2,0,1:T(8,128)(2,1)}, bf16[64,4,2048]{2,0,1:T(8,128)(2,1)S(1)}, u32[]{:S(2)}, u32[]{:S(2)}) %collective-permute-start.10) | collective-permute-done | bytes 1048608 | tf_op jit(solution)/shard_map/ppermute | solution.py:14
  446.9 3.6 fusion.42
  463.9 24.0 %all-gather.5.cloned.1.call-done = bf16[64,8,2048]{2,0,1:T(8,128)(2,1)} async-done(((bf16[64,2,2048]{2,0,1:T(8,128)(2,1)}), bf16[64,8,2048]{2,0,1:T(8,128)(2,1)}) %all-gather.5.cloned.1.call-update) | async-done | bytes 2097168 | tf_op jit(solution)/shard_map/all_gather | solution.py:114
  (249 shorter events, 172.6 us)
Async XLA Ops:
  6.5 373.4 %all-gather.3.cloned.1.call-start = ((), (), s32[]{:S(2)}) async-start(), calls=%async_computation | async-start | bytes 2621440 | tf_op jit(solution)/shard_map/all_gather | solution.py:109
  9.3 4.5 collective-permute-start
  17.7 52.4 %copy-start = (bf16[64,8,2048]{2,0,1:T(8,128)(2,1)}, bf16[64,8,2048]{2,0,1:T(8,128)(2,1)S(1)}, u32[]{:S(2)}) copy-start(bf16[64,8,2048]{2,0,1:T(8,128)(2,1)S(1)} %broadcast_select_fusion.1) | copy-start | bytes 6291460
  19.2 50.9 %collective-permute-start.1 = (bf16[64,4,2048]{2,0,1:T(8,128)(2,1)}, bf16[64,4,2048]{2,0,1:T(8,128)(2,1)}, u32[]{:S(2)}, u32[]{:S(2)}) collective-permute-start(bf16[64,4,2048]{2,0,1:T(8,128)(2,1)} %get-tuple-element.32), channel_id=1, source_target_pairs={{0,1},{1,2},{2,3},{3,4},{4,5},{5,6},{6,7},{8,9},{9,10},{10,11},{11... | collective-permute-start | bytes 3145736 | tf_op jit(solution)/shard_map/ppermute | solution.py:14
  24.9 45.2 %collective-permute-start.2 = (bf16[64,4,2048]{2,0,1:T(8,128)(2,1)}, bf16[64,4,2048]{2,0,1:T(8,128)(2,1)}, u32[]{:S(2)}, u32[]{:S(2)}) collective-permute-start(bf16[64,4,2048]{2,0,1:T(8,128)(2,1)} %get-tuple-element.31), channel_id=1, source_target_pairs={{1,0},{2,1},{3,2},{4,3},{5,4},{6,5},{7,6},{9,8},{10,9},{11,10},{12... | collective-permute-start | bytes 3145736 | tf_op jit(solution)/shard_map/ppermute | solution.py:17
  117.0 2.7 collective-permute-start.3
  121.5 49.9 %collective-permute-start.4 = (bf16[64,4,2048]{2,0,1:T(8,128)(2,1)}, bf16[64,4,2048]{2,0,1:T(8,128)(2,1)}, u32[]{:S(2)}, u32[]{:S(2)}) collective-permute-start(bf16[64,4,2048]{2,0,1:T(8,128)(2,1)} %get-tuple-element.28), channel_id=1, source_target_pairs={{0,1},{1,2},{2,3},{3,4},{4,5},{5,6},{6,7},{8,9},{9,10},{10,11},{11... | collective-permute-start | bytes 3145736 | tf_op jit(solution)/shard_map/ppermute | solution.py:14
  126.9 44.5 %collective-permute-start.5 = (bf16[64,4,2048]{2,0,1:T(8,128)(2,1)}, bf16[64,4,2048]{2,0,1:T(8,128)(2,1)}, u32[]{:S(2)}, u32[]{:S(2)}) collective-permute-start(bf16[64,4,2048]{2,0,1:T(8,128)(2,1)} %get-tuple-element.27), channel_id=1, source_target_pairs={{1,0},{2,1},{3,2},{4,3},{5,4},{6,5},{7,6},{9,8},{10,9},{11,10},{12... | collective-permute-start | bytes 3145736 | tf_op jit(solution)/shard_map/ppermute | solution.py:17
  216.9 2.7 collective-permute-start.6
  219.9 47.8 %collective-permute-start.7 = (bf16[64,8,2048]{2,0,1:T(8,128)(2,1)S(1)}, bf16[64,8,2048]{2,0,1:T(8,128)(2,1)}, u32[]{:S(2)}, u32[]{:S(2)}) collective-permute-start(bf16[64,8,2048]{2,0,1:T(8,128)(2,1)S(1)} %maximum_select_fusion.1), channel_id=1, source_target_pairs={{0,16},{8,24},{16,0},{24,8},{1,17},{9,25},{17,1},{25,9},{2,18},{10... | collective-permute-start | bytes 6291464 | tf_op jit(solution)/shard_map/ppermute | solution.py:23
  271.1 49.0 %collective-permute-start.8 = (bf16[64,4,2048]{2,0,1:T(8,128)(2,1)}, bf16[64,4,2048]{2,0,1:T(8,128)(2,1)S(1)}, u32[]{:S(2)}, u32[]{:S(2)}) collective-permute-start(bf16[64,4,2048]{2,0,1:T(8,128)(2,1)} %get-tuple-element.24), channel_id=1, source_target_pairs={{0,1},{1,2},{2,3},{3,4},{4,5},{5,6},{6,7},{8,9},{9,10},{10,11},{11... | collective-permute-start | bytes 3145736 | tf_op jit(solution)/shard_map/ppermute | solution.py:14
  275.6 44.6 %collective-permute-start.9 = (bf16[64,4,2048]{2,0,1:T(8,128)(2,1)}, bf16[64,4,2048]{2,0,1:T(8,128)(2,1)}, u32[]{:S(2)}, u32[]{:S(2)}) collective-permute-start(bf16[64,4,2048]{2,0,1:T(8,128)(2,1)} %get-tuple-element.23), channel_id=1, source_target_pairs={{1,0},{2,1},{3,2},{4,3},{5,4},{6,5},{7,6},{9,8},{10,9},{11,10},{12... | collective-permute-start | bytes 3145736 | tf_op jit(solution)/shard_map/ppermute | solution.py:17
  352.1 41.6 %copy-start.25 = (bf16[64,3,64]{2,0,1:T(8,128)(2,1)S(1)}, bf16[64,3,64]{2,0,1:T(8,128)(2,1)}, u32[]{:S(2)}) copy-start(bf16[64,3,64]{2,0,1:T(8,128)(2,1)} %get-tuple-element.48) | copy-start | bytes 73732
  352.1 42.3 %copy-start.24 = (bf16[64,3,64]{2,0,1:T(8,128)(2,1)S(1)}, bf16[64,3,64]{2,0,1:T(8,128)(2,1)}, u32[]{:S(2)}) copy-start(bf16[64,3,64]{2,0,1:T(8,128)(2,1)} %get-tuple-element.46) | copy-start | bytes 73732
  352.1 42.4 %copy-start.23 = (bf16[64,3,64]{2,0,1:T(8,128)(2,1)S(1)}, bf16[64,3,64]{2,0,1:T(8,128)(2,1)}, u32[]{:S(2)}) copy-start(bf16[64,3,64]{2,0,1:T(8,128)(2,1)} %get-tuple-element.45) | copy-start | bytes 73732
  352.1 42.5 %copy-start.22 = (bf16[64,3,64]{2,0,1:T(8,128)(2,1)S(1)}, bf16[64,3,64]{2,0,1:T(8,128)(2,1)}, u32[]{:S(2)}) copy-start(bf16[64,3,64]{2,0,1:T(8,128)(2,1)} %get-tuple-element.44) | copy-start | bytes 73732
  352.1 42.7 %copy-start.21 = (bf16[64,3,64]{2,0,1:T(8,128)(2,1)S(1)}, bf16[64,3,64]{2,0,1:T(8,128)(2,1)}, u32[]{:S(2)}) copy-start(bf16[64,3,64]{2,0,1:T(8,128)(2,1)} %get-tuple-element.43) | copy-start | bytes 73732
  352.2 42.8 %copy-start.20 = (bf16[64,3,64]{2,0,1:T(8,128)(2,1)S(1)}, bf16[64,3,64]{2,0,1:T(8,128)(2,1)}, u32[]{:S(2)}) copy-start(bf16[64,3,64]{2,0,1:T(8,128)(2,1)} %get-tuple-element.42) | copy-start | bytes 73732
  352.2 42.9 %copy-start.16 = (bf16[64,3,64]{2,0,1:T(8,128)(2,1)S(1)}, bf16[64,3,64]{2,0,1:T(8,128)(2,1)}, u32[]{:S(2)}) copy-start(bf16[64,3,64]{2,0,1:T(8,128)(2,1)} %get-tuple-element.60) | copy-start | bytes 73732
  352.2 43.0 %copy-start.19 = (bf16[64,3,64]{2,0,1:T(8,128)(2,1)S(1)}, bf16[64,3,64]{2,0,1:T(8,128)(2,1)}, u32[]{:S(2)}) copy-start(bf16[64,3,64]{2,0,1:T(8,128)(2,1)} %get-tuple-element.41) | copy-start | bytes 73732
  352.2 135.7 %all-gather.5.cloned.1.call-start = ((), (), s32[]{:S(2)}) async-start(), calls=%async_computation.1 | async-start | bytes 2621440 | tf_op jit(solution)/shard_map/all_gather | solution.py:114
  383.0 49.0 %collective-permute-start.10 = (bf16[64,4,2048]{2,0,1:T(8,128)(2,1)}, bf16[64,4,2048]{2,0,1:T(8,128)(2,1)S(1)}, u32[]{:S(2)}, u32[]{:S(2)}) collective-permute-start(bf16[64,4,2048]{2,0,1:T(8,128)(2,1)} %get-tuple-element.20), channel_id=1, source_target_pairs={{0,1},{1,2},{2,3},{3,4},{4,5},{5,6},{6,7},{8,9},{9,10},{10,11},{11... | collective-permute-start | bytes 3145736 | tf_op jit(solution)/shard_map/ppermute | solution.py:14
  386.4 45.5 %collective-permute-start.11 = (bf16[64,4,2048]{2,0,1:T(8,128)(2,1)}, bf16[64,4,2048]{2,0,1:T(8,128)(2,1)}, u32[]{:S(2)}, u32[]{:S(2)}) collective-permute-start(bf16[64,4,2048]{2,0,1:T(8,128)(2,1)} %get-tuple-element.19), channel_id=1, source_target_pairs={{1,0},{2,1},{3,2},{4,3},{5,4},{6,5},{7,6},{9,8},{10,9},{11,10},{12... | collective-permute-start | bytes 3145736 | tf_op jit(solution)/shard_map/ppermute | solution.py:17
  462.5 25.4 %copy-start.4 = (bf16[64,4,2048]{2,0,1:T(8,128)(2,1)S(1)}, bf16[64,4,2048]{2,0,1:T(8,128)(2,1)}, u32[]{:S(2)}) copy-start(bf16[64,4,2048]{2,0,1:T(8,128)(2,1)} %copy-done.3) | copy-start | bytes 3145732
  (42 other events, 238.8 us)
Sparse Core Ops, SparseCore 0:
  352.3 27.5 all-gather.2
  464.1 23.8 all-gather.4
where the time goes:
time: 507 us; the launch traced here: 500 us
  waiting for transfers between devices  249 us (49%)
  matrix products  111 us (22%)
  local copies, waits for them, and re-layouts  80.6 us (16%)
  starting transfers between devices  26.4 us (5%)
  other arithmetic  17.3 us (3%)
  between operations  15.3 us (3%)
    ppermute x4, waiting for transfers between devices, extended_2(): lax.ppermute(lax.slice_in_dim(block, block.shape[dim] - width, None, axis...  143 us
    dot_general x48, matrix products, conv_rows(): jnp.einsum('ok,khw->ohw', joined, stacked[:, shift_row:shift_row + row_co...  111 us
    ppermute x4, waiting for transfers between devices, partner_2(): lax.ppermute(x, axis, [(i, i ^ 1 << distance) for i in range(lax.axis_siz...  54.7 us
    slice x16, local copies, waits for them, and re-layouts, conv_rows(): padded[:, :, shift_col:shift_col + width]  34.2 us
    transpose x52, local copies, waits for them, and re-layouts, conv_rows(): jnp.transpose(kernel[shift_row], (1, 0, 2))  30.3 us
    all_gather x1, waiting for transfers between devices, local(): high_two = lax.all_gather(high_quarter, 'frame', axis=1, tiled=True)  27.6 us
    all_gather x1, waiting for transfers between devices, local(): low_two = lax.all_gather(low_quarter, 'frame', axis=1, tiled=True)  24 us
    ppermute x4, starting transfers between devices, extended_2(): lax.ppermute(lax.slice_in_dim(block, block.shape[dim] - width, None, axis...  18.9 us
  transfers between devices with their start and end apart: 14, of which 10 were waited for; matrix products, arithmetic and copies ran while one was open for 6% of the time, Pallas kernels for 0%

commit v1 on v0

v1 whole, which is shorter than its diff:
```python
import functools

import jax
import jax.numpy as jnp
from jax import lax
from jax.experimental import pallas as pl
from jax.experimental.pallas import tpu as pltpu
from jax.sharding import PartitionSpec as P

LANES = 128


def network_kernel(total_rows, sign, row_ref, x_ref, base_ref, w_ref, b_ref, out_ref, a_ref, c_ref):
    layers = w_ref.shape[0]
    rows, channels, width = x_ref.shape
    first_row = row_ref[0]
    column = lax.broadcasted_iota(jnp.int32, (2 * channels, width), 1)
    source = x_ref
    for layer in range(layers):
        rows -= 2
        last = layer == layers - 1
        target = out_ref if last else (a_ref, c_ref)[layer % 2]

        def pair(i, carry, source=source, target=target, layer=layer, last=last):
            x = source[pl.ds(2 * i, 4)].reshape(4 * channels, width)
            acc = jnp.dot(w_ref[layer], x, preferred_element_type=jnp.float32)
            group = 2 * channels
            left = pltpu.roll(acc[:group], 1, 1)
            right = pltpu.roll(acc[2 * group :], width - 1, 1)
            y = (
                acc[group : 2 * group]
                + jnp.where(column == 0, 0.0, left)
                + jnp.where(column == width - 1, 0.0, right)
                + b_ref[layer]
            )
            for p in range(2):
                part = y[p * channels : (p + 1) * channels]
                if last:
                    base = base_ref[2 * i + p].astype(jnp.float32)
                    part = base + part if sign > 0 else base - part
                else:
                    g = first_row + layer + 1 + 2 * i + p
                    inside = jnp.logical_and(g >= 0, g < total_rows)
                    part = jnp.where(inside, jnp.maximum(part, 0.0), 0.0)
                target[2 * i + p] = part.astype(jnp.bfloat16)
            return carry

        lax.fori_loop(0, rows // 2, pair, 0)
        source = target


def network(x, base, first_row, total_rows, weights, bias, sign):
    rows, channels, width = x.shape
    layers = weights.shape[0]
    macs = sum(rows - 2 * (k + 1) for k in range(layers)) * width * channels * channels * 12
    vmem = pl.BlockSpec(memory_space=pltpu.VMEM)
    return pl.pallas_call(
        functools.partial(network_kernel, total_rows, sign),
        out_shape=jax.ShapeDtypeStruct(base.shape, jnp.bfloat16),
        in_specs=[pl.BlockSpec(memory_space=pltpu.SMEM), vmem, vmem, vmem, vmem],
        out_specs=vmem,
        scratch_shapes=[
            pltpu.VMEM((rows - 2, channels, width), jnp.bfloat16),
            pltpu.VMEM((rows - 4, channels, width), jnp.bfloat16),
        ],
        compiler_params=pltpu.CompilerParams(vmem_limit_bytes=40 * 1024 * 1024),
        cost_estimate=pl.CostEstimate(
            flops=2 * macs, bytes_accessed=2 * (x.size + 2 * base.size), transcendentals=0
        ),
    )(first_row, x, base, weights, bias)


def pair_weights(kernels):
    lead = kernels.ndim - 4
    placed = []
    for p in range(2):
        pads = [(0, 0)] * kernels.ndim
        pads[lead] = (p, 1 - p)
        placed.append(jnp.pad(kernels, pads))
    stacked = jnp.stack(placed, axis=lead)
    order = tuple(range(lead)) + tuple(lead + k for k in (2, 0, 3, 1, 4))
    moved = jnp.transpose(stacked, order)
    shape = moved.shape
    return moved.reshape(
        shape[:lead] + (shape[lead] * shape[lead + 1] * shape[lead + 2], shape[lead + 3] * shape[lead + 4])
    )


def local(frames, predict_w, predict_b, update_w, update_b):
    layers = predict_w.shape[1]
    own = jnp.transpose(frames[0], (1, 0, 2))
    own_rows, channels, width = own.shape
    half = own_rows // 2
    frame_count = lax.axis_size("frame")
    tile_count = lax.axis_size("tile")
    total_rows = own_rows * tile_count
    position = lax.axis_index("frame")
    tile = lax.axis_index("tile")
    core = position % 2
    is_odd = core == 1
    upper = position // 2 % 2
    is_upper = upper == 1
    devices = [(f, t) for f in range(frame_count) for t in range(tile_count)]

    def send(x, target):
        pairs = []
        for f, t in devices:
            to = target(f, t)
            if to is not None and 0 <= to[1] < tile_count:
                pairs.append((f * tile_count + t, to[0] * tile_count + to[1]))
        return lax.ppermute(x, ("frame", "tile"), pairs)

    def swap_core(x):
        return send(x, lambda f, t: (f ^ 1, t))

    def swap_halo(x):
        return send(x, lambda f, t: (f ^ 1, t + 1 if f % 2 else t - 1))

    predict_m, update_m = pair_weights(predict_w), pair_weights(update_w)

    def wide_bias(b):
        return jnp.concatenate([b, b], axis=-1)[..., None]

    predict_v, update_v = wide_bias(predict_b), wide_bias(update_b)
    first_row = (tile * own_rows + core * half - layers).astype(jnp.int32)[None]

    def around(x, other, halo):
        return jnp.concatenate(
            [jnp.where(is_odd, other, halo), x, jnp.where(is_odd, halo, other)], axis=0
        )

    top, bottom = own[:half], own[half:]
    down = send(bottom, lambda f, t: (f, t + 1) if f % 2 == 0 else None)
    up = send(top, lambda f, t: (f + 1, t - 1) if f % 2 == 0 else None)
    got_top = swap_core(top)
    got_bottom = send(bottom, lambda f, t: (f + 1, t) if f % 2 == 0 else None)
    even_field = jnp.concatenate(
        [
            jnp.where(is_odd, got_top, down),
            jnp.where(is_odd, got_bottom, top),
            jnp.where(is_odd, up, bottom),
        ],
        axis=0,
    )
    odd_half = jnp.where(is_odd, bottom, got_top)
    even_half = even_field[layers : layers + half]
    high = network(even_field, odd_half, first_row, total_rows, predict_m[0], predict_v[0], -1)
    high_halo = swap_halo(high)
    high_other = swap_core(high)
    low = network(
        around(high, high_other, high_halo), even_half, first_row, total_rows,
        update_m[0], update_v[0], 1,
    )

    part = width // 2
    block = part + LANES
    give = jnp.where(is_upper, low[:, :, :block], low[:, :, width - block :])
    keep = jnp.where(is_upper, low[:, :, width - block :], low[:, :, :block])
    got = send(give, lambda f, t: (f ^ 2, t))
    low_even = jnp.where(is_upper, got, keep)
    low_odd = jnp.where(is_upper, keep, got)
    even_halo = swap_halo(low_even)
    even_other = swap_core(low_even)
    high_two = network(
        around(low_even, even_other, even_halo), low_odd, first_row, total_rows,
        predict_m[1], predict_v[1], -1,
    )
    two_halo = swap_halo(high_two)
    two_other = swap_core(high_two)

    def trimmed(x):
        return jnp.where(is_upper, x[:, :, block - part :], x[:, :, :part])

    high_mine, high_theirs = trimmed(high_two), trimmed(two_other)
    high_block = jnp.concatenate([high_mine, high_theirs], axis=0)
    high_left = send(high_block, lambda f, t: (f + 2, t) if f % 4 == 0 else None)
    low_two = network(
        around(high_two, two_other, two_halo), low_even, first_row, total_rows,
        update_m[1], update_v[1], 1,
    )
    low_mine = trimmed(low_two)
    low_theirs = send(low_mine, lambda f, t: (f - 1, t) if f % 4 == 1 else None)
    right_top = send(low_mine, lambda f, t: (f - 2, t) if f % 4 == 2 else None)
    right_bottom = send(low_mine, lambda f, t: (f - 3, t) if f % 4 == 3 else None)
    low_left = jnp.concatenate([low_mine, low_theirs], axis=0)
    low_right = jnp.concatenate([right_top, right_bottom], axis=0)
    second = jnp.concatenate(
        [jnp.where(is_upper, high_left, low_left), jnp.where(is_upper, high_block, low_right)], axis=2
    )
    first = jnp.concatenate([high_other, high], axis=0)
    chosen = jnp.where(is_odd, first, second)
    return jnp.transpose(chosen, (1, 0, 2))[None]


def solution(mesh):
    in_specs = (P("frame", None, "tile", None), P(), P(), P(), P())
    out_specs = P("frame", None, "tile", None)
    return jax.shard_map(local, mesh=mesh, in_specs=in_specs, out_specs=out_specs, check_vma=False)
```

time: 507 us -> 200 us (0.39)
  the two profiles are of different devices: /device:TPU:0 before, /device:TPU:6 now
where the time goes in v1:
time: 200 us; the launch traced here: 199 us
  waiting for transfers between devices  71.5 us (36%)
  local copies, waits for them, and re-layouts  43 us (22%)
  Pallas kernels  40.2 us (20%)
  starting transfers between devices  27.8 us (14%)
  other arithmetic  16.5 us (8%)
    ppermute x15, waiting for transfers between devices, send(): return lax.ppermute(x, ('frame', 'tile'), pairs)  71.5 us
    pallas_call x4, Pallas kernels, network(): pl.pallas_call(functools.partial(network_kernel, total_rows, sign), out_s...  40.2 us
    ppermute x15, starting transfers between devices, send(): return lax.ppermute(x, ('frame', 'tile'), pairs)  27.8 us
    slice x2, local copies, waits for them, and re-layouts, local(): update_m[1]  5.93 us
    slice x2, local copies, waits for them, and re-layouts, local(): predict_m[1]  5.92 us
    another operation x2, local copies, waits for them, and re-layouts, pair_weights(): stacked = jnp.stack(placed, axis=lead)  5.37 us
    unnamed x15, local copies, waits for them, and re-layouts  5.2 us
    select_n x3, other arithmetic, around(): jnp.where(is_odd, other, halo)  4.39 us
  transfers between devices with their start and end apart: 15, of which 8 were waited for; matrix products, arithmetic and copies ran while one was open for 19% of the time, Pallas kernels for 0%

profile of v1, /device:TPU:6, one launch (start us, length us, event | category | flops | bytes accessed | tf_op | source)
XLA Modules:
  0.0 199.4 jit_solution(13336258115099730703)
XLA Ops:
  0.0 2.7 %copy.33 = bf16[1,64,8,2048]{3,1,2,0:T(8,128)(2,1)S(1)} copy(bf16[1,64,8,2048]{3,2,1,0:T(8,128)(2,1)} %param.5) | data formatting | bytes 4194304 | tf_op args[0]
  3.9 2.8 %collective-permute-start.3 = (bf16[4,64,2048]{2,1,0:T(8,128)(2,1)}, bf16[4,64,2048]{2,1,0:T(8,128)(2,1)}, u32[]{:S(2)}, u32[]{:S(2)}) collective-permute-start(bf16[4,64,2048]{2,1,0:T(8,128)(2,1)} %slice.82), channel_id=1, source_target_pairs={{1,8},{2,9},{3,10},{4,11},{5,12},{6,13},{7,14},{17,24},{18,25},{19... | collective-permute-start | bytes 3145736 | tf_op jit(solution)/shard_map/ppermute | solution.py:111
  6.7 11.6 %collective-permute-done.3 = bf16[4,64,2048]{2,1,0:T(8,128)(2,1)} collective-permute-done((bf16[4,64,2048]{2,1,0:T(8,128)(2,1)}, bf16[4,64,2048]{2,1,0:T(8,128)(2,1)}, u32[]{:S(2)}, u32[]{:S(2)}) %collective-permute-start.3) | collective-permute-done | bytes 1048608 | tf_op jit(solution)/shard_map/ppermute | solution.py:111
  20.1 6.9 %collective-permute-start.2 = (bf16[4,64,2048]{2,1,0:T(8,128)(2,1)}, bf16[4,64,2048]{2,1,0:T(8,128)(2,1)}, u32[]{:S(2)}, u32[]{:S(2)}) collective-permute-start(bf16[4,64,2048]{2,1,0:T(8,128)(2,1)} %get-tuple-element.12), channel_id=1, source_target_pairs={{0,8},{1,9},{2,10},{3,11},{4,12},{5,13},{6,14},{7,15},{16,24},{17,... | collective-permute-start | bytes 3145736 | tf_op jit(solution)/shard_map/ppermute | solution.py:111
  27.3 2.7 %pad_bitcast_fusion.3 = (bf16[2,4,1,4,3,64,64]{6,5,4,3,1,0,2:T(8,128)(2,1)S(1)}, bf16[2,4,1,4,3,64,64]{6,5,4,3,1,0,2:T(8,128)(2,1)S(1)}) fusion(bf16[2,4,3,3,64,64]{5,4,3,2,1,0:T(8,128)(2,1)} %param.6), kind=kLoop, calls=%fused_computation.12 | loop fusion | bytes 2162688 | tf_op jit(solution)/shard_map/stack | solution.py:80
  37.7 2.8 %squeeze.28.w_ref = bf16[4,384,256]{2,1,0:T(8,128)(2,1)S(1)} reshape(bf16[1,4,3,2,64,4,64]{6,5,4,3,2,1,0:T(4,128)(2,1)} %copy.23) | data formatting | bytes 1572864 | tf_op jit(solution)/shard_map/squeeze | solution.py:147
  41.9 5.0 %collective-permute-done.1 = bf16[4,64,2048]{2,1,0:T(8,128)(2,1)} collective-permute-done((bf16[4,64,2048]{2,1,0:T(8,128)(2,1)}, bf16[4,64,2048]{2,1,0:T(8,128)(2,1)}, u32[]{:S(2)}, u32[]{:S(2)}) %collective-permute-start.1) | collective-permute-done | bytes 1048608 | tf_op jit(solution)/shard_map/ppermute | solution.py:111
  49.5 12.1 %shard_map.55 = bf16[4,64,2048]{2,1,0:T(8,128)(2,1)S(1)} custom-call(s32[1]{0:T(128)} %bitcast.row_ref, bf16[12,64,2048]{2,1,0:T(8,128)(2,1)S(1)} %pad_maximum_fusion.x_ref, bf16[4,64,2048]{2,1,0:T(8,128)(2,1)S(1)} %copy-done, bf16[4,384,256]{2,1,0:T(8,128)(2,1)S(1)} %squeeze.28.w_ref, f32[4,128,1]{2,1,0:T(8,128)S(1)} %copy.24.b_ref), custom_call_target="tpu_custom_call" | custom-call | flops 5637144576 | bytes 5242880 | tf_op jit(solution)/shard_map/pallas_call | solution.py:57
  65.6 2.7 %pad_bitcast_fusion.1 = (bf16[2,4,1,4,3,64,64]{6,5,4,3,1,0,2:T(8,128)(2,1)S(1)}, bf16[2,4,1,4,3,64,64]{6,5,4,3,1,0,2:T(8,128)(2,1)S(1)}) fusion(bf16[2,4,3,3,64,64]{5,4,3,2,1,0:T(8,128)(2,1)} %param.8), kind=kLoop, calls=%fused_computation.10 | loop fusion | bytes 2162688 | tf_op jit(solution)/shard_map/stack | solution.py:80
  70.9 2.6 %copy.25 = bf16[1,4,3,2,64,4,64]{6,5,4,3,2,1,0:T(4,128)(2,1)} copy(bf16[1,4,3,2,64,4,64]{6,4,2,5,1,0,3:T(8,128)(2,1)S(1)} %get-tuple-element.6) | data formatting | bytes 1572864 | tf_op jit(solution)/shard_map/slice | solution.py:152
  73.5 2.8 %squeeze.30.w_ref = bf16[4,384,256]{2,1,0:T(8,128)(2,1)S(1)} reshape(bf16[1,4,3,2,64,4,64]{6,5,4,3,2,1,0:T(4,128)(2,1)} %copy.25) | data formatting | bytes 1572864 | tf_op jit(solution)/shard_map/squeeze | solution.py:152
  76.3 12.7 %collective-permute-done.5 = bf16[4,64,2048]{2,1,0:T(8,128)(2,1)} collective-permute-done((bf16[4,64,2048]{2,1,0:T(8,128)(2,1)S(1)}, bf16[4,64,2048]{2,1,0:T(8,128)(2,1)}, u32[]{:S(2)}, u32[]{:S(2)}) %collective-permute-start.5) | collective-permute-done | bytes 1048608 | tf_op jit(solution)/shard_map/ppermute | solution.py:111
  91.1 12.1 %shard_map.56 = bf16[4,64,2048]{2,1,0:T(8,128)(2,1)S(1)} custom-call(s32[1]{0:T(128)} %bitcast.row_ref, bf16[12,64,2048]{2,1,0:T(8,128)(2,1)S(1)} %pad_maximum_fusion.1.x_ref, bf16[4,64,2048]{2,1,0:T(8,128)(2,1)S(1)} %broadcast_select_fusion.4.base_ref, bf16[4,384,256]{2,1,0:T(8,128)(2,1)S(1)} %squeeze.30.w_ref, f32[4,128,1]{2,1,0:T(8,128)S(1)} %copy.26.b_ref), custom_call_target="tpu_custom_call" | custom-call | flops 5637144576 | bytes 5242880 | tf_op jit(solution)/shard_map/pallas_call | solution.py:57
  103.9 9.4 %collective-permute-done.6 = bf16[4,64,1152]{2,1,0:T(8,128)(2,1)S(1)} collective-permute-done((bf16[4,64,1152]{2,1,0:T(8,128)(2,1)S(1)}, bf16[4,64,1152]{2,1,0:T(8,128)(2,1)S(1)}, u32[]{:S(2)}, u32[]{:S(2)}) %collective-permute-start.6) | collective-permute-done | bytes 589856 | tf_op jit(solution)/shard_map/ppermute | solution.py:111
  116.6 4.0 %copy.27 = bf16[1,4,3,2,64,4,64]{6,5,4,3,2,1,0:T(4,128)(2,1)} copy(bf16[1,4,3,2,64,4,64]{6,4,2,5,1,0,3:T(8,128)(2,1)} %get-tuple-element.7) | data formatting | bytes 1572864 | tf_op jit(solution)/shard_map/slice | solution.py:166
  120.6 2.8 %squeeze.32.w_ref = bf16[4,384,256]{2,1,0:T(8,128)(2,1)S(1)} reshape(bf16[1,4,3,2,64,4,64]{6,5,4,3,2,1,0:T(4,128)(2,1)} %copy.27) | data formatting | bytes 1572864 | tf_op jit(solution)/shard_map/squeeze | solution.py:166
  128.6 8.0 %shard_map.57 = bf16[4,64,1152]{2,1,0:T(8,128)(2,1)S(1)} custom-call(s32[1]{0:T(128)} %bitcast.row_ref, bf16[12,64,1152]{2,1,0:T(8,128)(2,1)S(1)} %pad_maximum_fusion.2.x_ref, bf16[4,64,1152]{2,1,0:T(8,128)(2,1)S(1)} %copy-done.1, bf16[4,384,256]{2,1,0:T(8,128)(2,1)S(1)} %squeeze.32.w_ref, f32[4,128,1]{2,1,0:T(8,128)S(1)} %copy.28.b_ref), custom_call_target="tpu_custom_call" | custom-call | flops 3170893824 | bytes 2949120 | tf_op jit(solution)/shard_map/pallas_call | solution.py:57
  140.1 4.0 %copy.29 = bf16[1,4,3,2,64,4,64]{6,5,4,3,2,1,0:T(4,128)(2,1)} copy(bf16[1,4,3,2,64,4,64]{6,4,2,5,1,0,3:T(8,128)(2,1)} %get-tuple-element.5) | data formatting | bytes 1572864 | tf_op jit(solution)/shard_map/slice | solution.py:179
  144.1 2.8 %squeeze.34.w_ref = bf16[4,384,256]{2,1,0:T(8,128)(2,1)S(1)} reshape(bf16[1,4,3,2,64,4,64]{6,5,4,3,2,1,0:T(4,128)(2,1)} %copy.29) | data formatting | bytes 1572864 | tf_op jit(solution)/shard_map/squeeze | solution.py:179
  147.0 7.1 %collective-permute-done.11 = bf16[4,64,1152]{2,1,0:T(8,128)(2,1)} collective-permute-done((bf16[4,64,1152]{2,1,0:T(8,128)(2,1)S(1)}, bf16[4,64,1152]{2,1,0:T(8,128)(2,1)}, u32[]{:S(2)}, u32[]{:S(2)}) %collective-permute-start.11) | collective-permute-done | bytes 589856 | tf_op jit(solution)/shard_map/ppermute | solution.py:111
  155.6 8.0 %shard_map.58 = bf16[4,64,1152]{2,1,0:T(8,128)(2,1)S(1)} custom-call(s32[1]{0:T(128)} %bitcast.row_ref, bf16[12,64,1152]{2,1,0:T(8,128)(2,1)S(1)} %pad_maximum_fusion.3.x_ref, bf16[4,64,1152]{2,1,0:T(8,128)(2,1)S(1)} %get-tuple-element.15.base_ref, bf16[4,384,256]{2,1,0:T(8,128)(2,1)S(1)} %squeeze.34.w_ref, f32[4,128,1]{2,1,0:T(8,128)S(1)} %copy.30.b_ref), custom_call_target="tpu_custom_call" | custom-call | flops 3170893824 | bytes 2949120 | tf_op jit(solution)/shard_map/pallas_call | solution.py:57
  164.5 3.1 %collective-permute-start.13 = (bf16[4,64,1024]{2,1,0:T(8,128)(2,1)S(1)}, bf16[4,64,1024]{2,1,0:T(8,128)(2,1)S(1)}, u32[]{:S(2)}, u32[]{:S(2)}) collective-permute-start(bf16[4,64,1024]{2,1,0:T(8,128)(2,1)S(1)} %slice_select_fusion), channel_id=1, source_target_pairs={{16,0},{17,1},{18,2},{19,3},{20,4},{21,5},{22,6},{23,7}} | collective-permute-start | bytes 1572872 | tf_op jit(solution)/shard_map/ppermute | solution.py:111
  168.9 9.0 %collective-permute-done.13 = bf16[4,64,1024]{2,1,0:T(8,128)(2,1)S(1)} collective-permute-done((bf16[4,64,1024]{2,1,0:T(8,128)(2,1)S(1)}, bf16[4,64,1024]{2,1,0:T(8,128)(2,1)S(1)}, u32[]{:S(2)}, u32[]{:S(2)}) %collective-permute-start.13) | collective-permute-done | bytes 524320 | tf_op jit(solution)/shard_map/ppermute | solution.py:111
  180.1 14.7 %collective-permute-done.10 = bf16[8,64,1024]{2,1,0:T(8,128)(2,1)S(1)} collective-permute-done((bf16[8,64,1024]{2,1,0:T(8,128)(2,1)S(1)}, bf16[8,64,1024]{2,1,0:T(8,128)(2,1)S(1)}, u32[]{:S(2)}, u32[]{:S(2)}) %collective-permute-start.10) | collective-permute-done | bytes 1048608 | tf_op jit(solution)/shard_map/ppermute | solution.py:111
  (65 shorter events, 46.5 us)
Async XLA Ops:
  2.7 17.4 %copy-start.2 = (bf16[1,64,8,2048]{3,1,2,0:T(8,128)(2,1)}, bf16[1,64,8,2048]{3,1,2,0:T(8,128)(2,1)S(1)}, u32[]{:S(2)}) copy-start(bf16[1,64,8,2048]{3,1,2,0:T(8,128)(2,1)S(1)} %copy.33) | copy-start | bytes 6291460
  3.9 14.5 %collective-permute-start.3 = (bf16[4,64,2048]{2,1,0:T(8,128)(2,1)}, bf16[4,64,2048]{2,1,0:T(8,128)(2,1)}, u32[]{:S(2)}, u32[]{:S(2)}) collective-permute-start(bf16[4,64,2048]{2,1,0:T(8,128)(2,1)} %slice.82), channel_id=1, source_target_pairs={{1,8},{2,9},{3,10},{4,11},{5,12},{6,13},{7,14},{17,24},{18,25},{19... | collective-permute-start | bytes 3145736 | tf_op jit(solution)/shard_map/ppermute | solution.py:111
  6.7 11.6 %collective-permute-start = (bf16[4,64,2048]{2,1,0:T(8,128)(2,1)}, bf16[4,64,2048]{2,1,0:T(8,128)(2,1)S(1)}, u32[]{:S(2)}, u32[]{:S(2)}) collective-permute-start(bf16[4,64,2048]{2,1,0:T(8,128)(2,1)} %slice.82), channel_id=1, source_target_pairs={{0,8},{1,9},{2,10},{3,11},{4,12},{5,13},{6,14},{7,15},{8,0},{9,1},... | collective-permute-start | bytes 3145736 | tf_op jit(solution)/shard_map/ppermute | solution.py:111
  6.7 20.3 %copy-start.5 = (f32[2,4,64]{2,1,0:T(4,128)S(1)}, f32[2,4,64]{2,1,0:T(4,128)}, u32[]{:S(2)}) copy-start(f32[2,4,64]{2,1,0:T(4,128)} %param.7) | copy-start | bytes 6148
  20.1 20.4 %collective-permute-start.2 = (bf16[4,64,2048]{2,1,0:T(8,128)(2,1)}, bf16[4,64,2048]{2,1,0:T(8,128)(2,1)}, u32[]{:S(2)}, u32[]{:S(2)}) collective-permute-start(bf16[4,64,2048]{2,1,0:T(8,128)(2,1)} %get-tuple-element.12), channel_id=1, source_target_pairs={{0,8},{1,9},{2,10},{3,11},{4,12},{5,13},{6,14},{7,15},{16,24},{17,... | collective-permute-start | bytes 3145736 | tf_op jit(solution)/shard_map/ppermute | solution.py:111
  29.9 17.0 %collective-permute-start.1 = (bf16[4,64,2048]{2,1,0:T(8,128)(2,1)}, bf16[4,64,2048]{2,1,0:T(8,128)(2,1)}, u32[]{:S(2)}, u32[]{:S(2)}) collective-permute-start(bf16[4,64,2048]{2,1,0:T(8,128)(2,1)} %get-tuple-element.12), channel_id=1, source_target_pairs={{0,1},{1,2},{2,3},{3,4},{4,5},{5,6},{6,7},{16,17},{17,18},{18,19},... | collective-permute-start | bytes 3145736 | tf_op jit(solution)/shard_map/ppermute | solution.py:111
  41.9 6.4 %copy-start.3 = (bf16[4,64,2048]{2,1,0:T(8,128)(2,1)S(1)}, bf16[4,64,2048]{2,1,0:T(8,128)(2,1)}, u32[]{:S(2)}) copy-start(bf16[4,64,2048]{2,1,0:T(8,128)(2,1)} %get-tuple-element.13) | copy-start | bytes 3145732
  48.3 1.2 copy-start
  49.5 15.9 %copy-start.6 = (f32[2,4,64]{2,1,0:T(4,128)S(1)}, f32[2,4,64]{2,1,0:T(4,128)}, u32[]{:S(2)}) copy-start(f32[2,4,64]{2,1,0:T(4,128)} %param.9) | copy-start | bytes 6148
  61.6 27.5 %collective-permute-start.5 = (bf16[4,64,2048]{2,1,0:T(8,128)(2,1)S(1)}, bf16[4,64,2048]{2,1,0:T(8,128)(2,1)}, u32[]{:S(2)}, u32[]{:S(2)}) collective-permute-start(bf16[4,64,2048]{2,1,0:T(8,128)(2,1)S(1)} %shard_map.55), channel_id=1, source_target_pairs={{1,8},{2,9},{3,10},{4,11},{5,12},{6,13},{7,14},{8,1},{9,2},{10,3},... | collective-permute-start | bytes 3145736 | tf_op jit(solution)/shard_map/ppermute | solution.py:111
  63.7 25.4 %collective-permute-start.4 = (bf16[4,64,2048]{2,1,0:T(8,128)(2,1)S(1)}, bf16[4,64,2048]{2,1,0:T(8,128)(2,1)}, u32[]{:S(2)}, u32[]{:S(2)}) collective-permute-start(bf16[4,64,2048]{2,1,0:T(8,128)(2,1)S(1)} %shard_map.55), channel_id=1, source_target_pairs={{0,8},{1,9},{2,10},{3,11},{4,12},{5,13},{6,14},{7,15},{8,0},{9,1},... | collective-permute-start | bytes 3145736 | tf_op jit(solution)/shard_map/ppermute | solution.py:111
  103.3 9.9 %collective-permute-start.6 = (bf16[4,64,1152]{2,1,0:T(8,128)(2,1)S(1)}, bf16[4,64,1152]{2,1,0:T(8,128)(2,1)S(1)}, u32[]{:S(2)}, u32[]{:S(2)}) collective-permute-start(bf16[4,64,1152]{2,1,0:T(8,128)(2,1)S(1)} %broadcast_select_fusion.9), channel_id=1, source_target_pairs={{0,16},{1,17},{2,18},{3,19},{4,20},{5,21},{6,22},{7,23},{8,24},{9,... | collective-permute-start | bytes 1769480 | tf_op jit(solution)/shard_map/ppermute | solution.py:111
  114.2 11.2 %collective-permute-start.8 = (bf16[4,64,1152]{2,1,0:T(8,128)(2,1)S(1)}, bf16[4,64,1152]{2,1,0:T(8,128)(2,1)S(1)}, u32[]{:S(2)}, u32[]{:S(2)}) collective-permute-start(bf16[4,64,1152]{2,1,0:T(8,128)(2,1)S(1)} %get-tuple-element.15.base_ref), channel_id=1, source_target_pairs={{1,8},{2,9},{3,10},{4,11},{5,12},{6,13},{7,14},{8,1},{9,2},{10,3},... | collective-permute-start | bytes 1769480 | tf_op jit(solution)/shard_map/ppermute | solution.py:111
  116.3 9.9 %collective-permute-start.7 = (bf16[4,64,1152]{2,1,0:T(8,128)(2,1)S(1)}, bf16[4,64,1152]{2,1,0:T(8,128)(2,1)}, u32[]{:S(2)}, u32[]{:S(2)}) collective-permute-start(bf16[4,64,1152]{2,1,0:T(8,128)(2,1)S(1)} %get-tuple-element.15.base_ref), channel_id=1, source_target_pairs={{0,8},{1,9},{2,10},{3,11},{4,12},{5,13},{6,14},{7,15},{8,0},{9,1},... | collective-permute-start | bytes 1769480 | tf_op jit(solution)/shard_map/ppermute | solution.py:111
  125.4 0.8 copy-start.4
  127.6 1.1 copy-start.1
  136.7 17.3 %collective-permute-start.11 = (bf16[4,64,1152]{2,1,0:T(8,128)(2,1)S(1)}, bf16[4,64,1152]{2,1,0:T(8,128)(2,1)}, u32[]{:S(2)}, u32[]{:S(2)}) collective-permute-start(bf16[4,64,1152]{2,1,0:T(8,128)(2,1)S(1)} %shard_map.57), channel_id=1, source_target_pairs={{1,8},{2,9},{3,10},{4,11},{5,12},{6,13},{7,14},{8,1},{9,2},{10,3},... | collective-permute-start | bytes 1769480 | tf_op jit(solution)/shard_map/ppermute | solution.py:111
  138.6 15.4 %collective-permute-start.9 = (bf16[4,64,1152]{2,1,0:T(8,128)(2,1)S(1)}, bf16[4,64,1152]{2,1,0:T(8,128)(2,1)}, u32[]{:S(2)}, u32[]{:S(2)}) collective-permute-start(bf16[4,64,1152]{2,1,0:T(8,128)(2,1)S(1)} %shard_map.57), channel_id=1, source_target_pairs={{0,8},{1,9},{2,10},{3,11},{4,12},{5,13},{6,14},{7,15},{8,0},{9,1},... | collective-permute-start | bytes 1769480 | tf_op jit(solution)/shard_map/ppermute | solution.py:111
  163.8 5.1 %collective-permute-start.14 = (bf16[4,64,1024]{2,1,0:T(8,128)(2,1)S(1)}, bf16[4,64,1024]{2,1,0:T(8,128)(2,1)S(1)}, u32[]{:S(2)}, u32[]{:S(2)}) collective-permute-start(bf16[4,64,1024]{2,1,0:T(8,128)(2,1)S(1)} %slice_select_fusion), channel_id=1, source_target_pairs={{24,0},{25,1},{26,2},{27,3},{28,4},{29,5},{30,6},{31,7}} | collective-permute-start | bytes 1572872 | tf_op jit(solution)/shard_map/ppermute | solution.py:111
  164.5 13.5 %collective-permute-start.13 = (bf16[4,64,1024]{2,1,0:T(8,128)(2,1)S(1)}, bf16[4,64,1024]{2,1,0:T(8,128)(2,1)S(1)}, u32[]{:S(2)}, u32[]{:S(2)}) collective-permute-start(bf16[4,64,1024]{2,1,0:T(8,128)(2,1)S(1)} %slice_select_fusion), channel_id=1, source_target_pairs={{16,0},{17,1},{18,2},{19,3},{20,4},{21,5},{22,6},{23,7}} | collective-permute-start | bytes 1572872 | tf_op jit(solution)/shard_map/ppermute | solution.py:111
  178.1 16.7 %collective-permute-start.10 = (bf16[8,64,1024]{2,1,0:T(8,128)(2,1)S(1)}, bf16[8,64,1024]{2,1,0:T(8,128)(2,1)S(1)}, u32[]{:S(2)}, u32[]{:S(2)}) collective-permute-start(bf16[8,64,1024]{2,1,0:T(8,128)(2,1)S(1)} %get-tuple-element.24), channel_id=1, source_target_pairs={{0,16},{1,17},{2,18},{3,19},{4,20},{5,21},{6,22},{7,23}} | collective-permute-start | bytes 3145736 | tf_op jit(solution)/shard_map/ppermute | solution.py:111
  179.4 0.7 collective-permute-start.12

commit v2 on v0

v2 whole, which is shorter than its diff:
```python
import functools

import jax
import jax.numpy as jnp
from jax import lax
from jax.experimental import pallas as pl
from jax.experimental.pallas import tpu as pltpu
from jax.sharding import PartitionSpec as P

LANES = 128
MESSAGES = (
    "down0", "down1", "up0", "up1", "even0", "even1", "odd",
    "hs0", "hs1", "hh0", "hh1", "x", "fs", "fh", "gs", "gh", "hl", "l1", "l2", "l3",
)
SLOT = {name: k for k, name in enumerate(MESSAGES)}
LOCAL = ("own", "base", "keep", "out", "out2")
LSLOT = {name: k for k, name in enumerate(LOCAL)}


def build_weights(k_ref, level, w_ref):
    layers, channels = k_ref.shape[1], k_ref.shape[5]
    w_ref[...] = jnp.zeros_like(w_ref)
    for layer in range(layers):
        for s in range(3):
            for p in range(2):
                top = (2 * s + p) * channels
                for r in range(3):
                    q = r + p
                    w_ref[layer, top : top + channels, q * channels : (q + 1) * channels] = k_ref[
                        level, layer, r, s
                    ]


def kernel(tiles, own, pw, uw, pb, ub, out, e, h, b1, low, f2, h2, o2, l2, wa, wb, wc, wd, a_ref, c_ref, send_sem, recv_sem, local_sem):
    own_rows, channels, width = own.shape
    half = own_rows // 2
    layers = pw.shape[1]
    part = width // 2
    block = part + LANES
    f = lax.axis_index("frame")
    t = lax.axis_index("tile")
    core = lax.rem(f, 2)
    upper = lax.rem(lax.div(f, 2), 2)
    partner = f + 1 - 2 * core
    across = f + 2 - 4 * upper
    diagonal = across + 1 - 2 * core
    has_up, has_down = t > 0, t < tiles - 1
    is_even, is_odd = core == 0, core == 1
    is_lower, is_upper = upper == 0, upper == 1
    first_row = t * own_rows + core * half - layers
    halo_tile = t + 2 * core - 1
    has_halo = jnp.logical_and(halo_tile >= 0, halo_tile < tiles)

    barrier = pltpu.get_barrier_semaphore()

    def greet(frame, tile):
        pl.semaphore_signal(
            barrier, inc=1, device_id={"frame": frame, "tile": tile},
            device_id_type=pl.DeviceIdType.MESH,
        )

    for frame in (partner, across, diagonal):
        greet(frame, t)
    for ok, tile in ((has_up, t - 1), (has_down, t + 1)):

        @pl.when(ok)
        def _(tile=tile):
            greet(f, tile)
            greet(partner, tile)

    def remote(name, src, dst, frame, tile):
        return pltpu.make_async_remote_copy(
            src_ref=src, dst_ref=dst, send_sem=send_sem.at[SLOT[name]], recv_sem=recv_sem.at[SLOT[name]],
            device_id={"frame": frame, "tile": tile}, device_id_type=pl.DeviceIdType.MESH,
        )

    def here(name, src, dst):
        return pltpu.make_async_copy(src, dst, local_sem.at[LSLOT[name]])

    @pl.when(jnp.logical_not(has_halo))
    def _():
        for ref in (e, h, f2, h2):
            ref[pl.ds(2 * half * core, half)] = jnp.zeros(
                (half,) + ref.shape[1:], ref.dtype
            )

    pl.semaphore_wait(barrier, 3 + 2 * has_up.astype(jnp.int32) + 2 * has_down.astype(jnp.int32))

    cut = (slice(0, block + LANES), slice(block + LANES, width))
    mine = slice(half, 2 * half)

    def downs(k):
        return remote(f"down{k}", own.at[half:, :, cut[k]], e.at[:half, :, cut[k]], f, t + 1)

    def ups(k):
        return remote(f"up{k}", own.at[:half, :, cut[k]], e.at[2 * half :, :, cut[k]], partner, t - 1)

    def evens(k):
        return remote(f"even{k}", own.at[:, :, cut[k]], e.at[: 2 * half, :, cut[k]], partner, t)

    odd = remote("odd", own.at[:half], b1, partner, t)
    own_copy = here("own", own, e.at[half:])
    base_copy = here("base", own.at[half:], b1)

    @pl.when(is_even)
    def _():
        for k in range(2):
            @pl.when(has_down)
            def _():
                downs(k).start()

            @pl.when(has_up)
            def _():
                ups(k).start()

            evens(k).start()
        own_copy.start()

    @pl.when(is_odd)
    def _():
        odd.start()
        base_copy.start()

    build_weights(pw, 0, wa)
    build_weights(uw, 0, wb)
    build_weights(pw, 1, wc)
    build_weights(uw, 1, wd)

    def network(src, base, dst, cols, keep, w_ref, b_ref, level, sign):
        size = cols.stop - cols.start
        column = lax.broadcasted_iota(jnp.int32, (1, size), 1)
        first, final = column == 0, column == size - 1
        rows = src.shape[0]
        source = src
        for layer in range(layers):
            rows -= 2
            last = layer == layers - 1
            target = dst if last else (a_ref, c_ref)[layer % 2]

            def pair(i, carry, source=source, target=target, layer=layer, last=last):
                span = cols if layer == 0 else slice(0, size)
                x = source[pl.ds(2 * i, 4), :, span].reshape(4 * channels, size)
                acc = jnp.dot(w_ref[layer], x, preferred_element_type=jnp.float32)
                group = 2 * channels
                left = pltpu.roll(acc[:group], 1, 1)
                right = pltpu.roll(acc[2 * group :], size - 1, 1)
                y = (
                    acc[group : 2 * group]
                    + jnp.where(first, 0.0, left)
                    + jnp.where(final, 0.0, right)
                    + b_ref[level, layer]
                )
                for p in range(2):
                    value = y[p * channels : (p + 1) * channels]
                    if last:
                        value = value[:, keep.start - cols.start : keep.stop - cols.start]
                        old = base[2 * i + p, :, keep].astype(jnp.float32)
                        value = old + value if sign > 0 else old - value
                        target[2 * i + p, :, keep] = value.astype(jnp.bfloat16)
                    else:
                        g = first_row + layer + 1 + 2 * i + p
                        inside = jnp.logical_and(g >= 0, g < tiles * own_rows)
                        value = jnp.where(inside, jnp.maximum(value, 0.0), 0.0)
                        target[2 * i + p, :, 0:size] = value.astype(jnp.bfloat16)
                return carry

            lax.fori_loop(0, rows // 2, pair, 0)
            source = target

    def swap(name, field, cols):
        piece = field.at[mine, :, cols]
        return remote(name, piece, field.at[pl.ds(2 * half * core, half), :, cols], partner, t)

    def swap_in(name, field, cols):
        piece = field.at[mine, :, cols]
        return remote(name, piece, field.at[pl.ds(2 * half * (1 - core), half), :, cols], partner, t)

    def halo(name, field, cols):
        piece = field.at[mine, :, cols]
        return remote(name, piece, field.at[pl.ds(2 * half * (1 - core), half), :, cols], partner, halo_tile)

    def halo_in(name, field, cols):
        piece = field.at[mine, :, cols]
        return remote(name, piece, field.at[pl.ds(2 * half * core, half), :, cols], partner, halo_tile)

    def share(kind, k, field, cols):
        @pl.when(has_halo)
        def _():
            halo(kind + "h" + k, field, cols).start()

        swap(kind + "s" + k, field, cols).start()

    def arrive(kind, k, field, cols):
        swap_in(kind + "s" + k, field, cols).wait_recv()

        @pl.when(has_halo)
        def _():
            halo_in(kind + "h" + k, field, cols).wait_recv()

    def sent(kind, k, field, cols):
        swap(kind + "s" + k, field, cols).wait_send()

        @pl.when(has_halo)
        def _():
            halo(kind + "h" + k, field, cols).wait_send()

    hcut = (slice(0, block), slice(block, width))
    for k in range(2):
        @pl.when(is_even)
        def _():
            if k == 0:
                own_copy.wait()
                odd.wait_recv()

            @pl.when(has_up)
            def _():
                downs(k).wait_recv()

        @pl.when(is_odd)
        def _():
            if k == 0:
                base_copy.wait()
            evens(k).wait_recv()

            @pl.when(has_down)
            def _():
                ups(k).wait_recv()

        reads = slice(0, block + LANES) if k == 0 else slice(part, width)
        network(e, b1, h.at[mine], reads, hcut[k], wa, pb, 0, -1)
        share("h", str(k), h, hcut[k])

    for k in range(2):
        arrive("h", str(k), h, hcut[k])
        reads = slice(0, block) if k == 0 else slice(width - block, width)
        keep = slice(0, part) if k == 0 else slice(part, width)
        network(h, e.at[mine], low, reads, keep, wb, ub, 0, 1)

    high_out = here("out", h.at[: 2 * half], out)
    left, right = slice(0, block), slice(width - block, width)
    give_even = remote("x", low.at[:, :, right], f2.at[mine], across, t)
    give_odd = remote("x", low.at[:, :, left], o2, across, t)
    keep_even = here("keep", low.at[:, :, left], f2.at[mine])
    keep_odd = here("keep", low.at[:, :, right], o2)
    every = slice(0, block)

    @pl.when(is_lower)
    def _():
        give_even.start()
        keep_even.start()
        keep_even.wait()

    @pl.when(is_upper)
    def _():
        give_odd.start()
        keep_odd.start()
        give_even.wait_recv()

    share("f", "", f2, every)

    @pl.when(is_odd)
    def _():
        high_out.start()

    arrive("f", "", f2, every)

    @pl.when(is_lower)
    def _():
        give_odd.wait_recv()

    @pl.when(is_upper)
    def _():
        keep_odd.wait()

    network(f2, o2, h2.at[mine], every, every, wc, pb, 1, -1)
    share("g", "", h2, every)
    arrive("g", "", h2, every)

    near, far = slice(0, part), slice(part, width)
    tail = slice(block - part, block)
    high_send = remote("hl", h2.at[half:, :, near], out.at[:, :, near], across, t)
    high_keep = here("out", h2.at[half:, :, tail], out.at[:, :, far])
    at_low = jnp.logical_and(is_even, is_lower)
    at_high = jnp.logical_and(is_even, is_upper)

    @pl.when(at_low)
    def _():
        high_send.start()

    @pl.when(at_high)
    def _():
        high_keep.start()

    network(h2, f2.at[mine], l2, every, every, wd, ub, 1, 1)

    low_keep = here("out2", l2.at[:, :, near], out.at[:half, :, near])
    first = remote("l1", l2.at[:, :, near], out.at[half:, :, near], partner, t)
    second = remote("l2", l2.at[:, :, tail], out.at[:half, :, far], across, t)
    third = remote("l3", l2.at[:, :, tail], out.at[half:, :, far], diagonal, t)

    @pl.when(at_low)
    def _():
        low_keep.start()
        first.wait_recv()
        second.wait_recv()
        third.wait_recv()
        low_keep.wait()
        high_send.wait_send()

    @pl.when(at_high)
    def _():
        second.start()
        high_keep.wait()
        high_send.wait_recv()
        second.wait_send()

    @pl.when(jnp.logical_and(is_odd, is_lower))
    def _():
        first.start()
        first.wait_send()

    @pl.when(jnp.logical_and(is_odd, is_upper))
    def _():
        third.start()
        third.wait_send()

    @pl.when(is_odd)
    def _():
        high_out.wait()
        odd.wait_send()

    @pl.when(is_even)
    def _():
        for k in range(2):
            @pl.when(has_down)
            def _():
                downs(k).wait_send()

            @pl.when(has_up)
            def _():
                ups(k).wait_send()

            evens(k).wait_send()

    @pl.when(is_lower)
    def _():
        give_even.wait_send()

    @pl.when(is_upper)
    def _():
        give_odd.wait_send()

    for k in range(2):
        sent("h", str(k), h, hcut[k])
    sent("f", "", f2, every)
    sent("g", "", h2, every)


def local(frames, predict_w, predict_b, update_w, update_b):
    own = jnp.transpose(frames[0], (1, 0, 2))
    own_rows, channels, width = own.shape
    half = own_rows // 2
    layers = predict_w.shape[1]
    block = width // 2 + LANES
    tiles = lax.axis_size("tile")

    def wide_bias(b):
        return jnp.concatenate([b, b], axis=-1)[..., None]

    vmem = pl.BlockSpec(memory_space=pltpu.VMEM)
    hbm = pl.BlockSpec(memory_space=pl.ANY)

    def buffer(rows, columns):
        return pltpu.VMEM((rows, channels, columns), jnp.bfloat16)

    weight = pltpu.VMEM((layers, 6 * channels, 4 * channels), jnp.bfloat16)
    result = pl.pallas_call(
        functools.partial(kernel, tiles),
        out_shape=jax.ShapeDtypeStruct(own.shape, jnp.bfloat16),
        in_specs=[hbm, vmem, vmem, vmem, vmem],
        out_specs=hbm,
        scratch_shapes=[
            buffer(3 * half, width), buffer(3 * half, width), buffer(half, width), buffer(half, width),
            buffer(3 * half, block), buffer(3 * half, block), buffer(half, block), buffer(half, block),
            weight, weight, weight, weight,
            buffer(3 * half - 2, block + LANES), buffer(3 * half - 4, block + LANES),
            pltpu.SemaphoreType.DMA((len(MESSAGES),)),
            pltpu.SemaphoreType.DMA((len(MESSAGES),)),
            pltpu.SemaphoreType.DMA((len(LOCAL),)),
        ],
        compiler_params=pltpu.CompilerParams(
            collective_id=0, has_side_effects=True, vmem_limit_bytes=60 * 1024 * 1024
        ),
    )(own, predict_w, update_w, wide_bias(predict_b), wide_bias(update_b))
    return jnp.transpose(result, (1, 0, 2))[None]


def solution(mesh):
    in_specs = (P("frame", None, "tile", None), P(), P(), P(), P())
    out_specs = P("frame", None, "tile", None)
    return jax.shard_map(local, mesh=mesh, in_specs=in_specs, out_specs=out_specs, check_vma=False)
```

time: 507 us -> 131 us (0.26); the launches traced: 500 us -> 131 us
  waiting for transfers between devices: 249 us -> 0 us
  Pallas kernels: 0 us -> 119 us
  matrix products: 111 us -> 0 us
  local copies, waits for them, and re-layouts: 80.6 us -> 10.2 us
  starting transfers between devices: 26.4 us -> 0 us
  other arithmetic: 17.3 us -> 1.67 us
  between operations: 15.3 us -> 0.01 us
    ppermute x12 -> x0, waiting for transfers between devices: 197 us -> none  [the longest x4 143 us: extended_2(): lax.ppermute(lax.slice_in_dim(block, block.shape[dim] - width, None, axis...]
    pallas_call x0 -> x1, Pallas kernels: none -> 119 us  [local(): pl.pallas_call(functools.partial(kernel, tiles), out_shape=jax.ShapeDtype...]
    dot_general x48 -> x0, matrix products: 111 us -> none  [conv_rows(): jnp.einsum('ok,khw->ohw', joined, stacked[:, shift_row:shift_row + row_co...]
    all_gather x2 -> x0, waiting for transfers between devices: 51.6 us -> none  [the longest x1 27.6 us: local(): high_two = lax.all_gather(high_quarter, 'frame', axis=1, tiled=True)]
    slice x20 -> x0, local copies, waits for them, and re-layouts: 41.7 us -> none  [the longest x16 34.2 us: conv_rows(): padded[:, :, shift_col:shift_col + width]]
    transpose x52 -> x0, local copies, waits for them, and re-layouts: 30.3 us -> none  [conv_rows(): jnp.transpose(kernel[shift_row], (1, 0, 2))]
    ppermute x12 -> x0, starting transfers between devices: 26.3 us -> none  [the longest x4 18.9 us: extended_2(): lax.ppermute(lax.slice_in_dim(block, block.shape[dim] - width, None, axis...]
    concatenate x4 -> x0, other arithmetic: 8.53 us -> none  [extended_2(): block = jnp.concatenate([low, block, high], axis=dim)]
  transfers between devices with their start and end apart: 14 -> 0, of which waited for: 10 -> 0; matrix products, arithmetic and copies ran while one was open for 6% -> 0% of each run, Pallas kernels for 0% -> 0%
where the time goes in v2:
time: 131 us
  Pallas kernels  119 us (91%)
  local copies, waits for them, and re-layouts  10.2 us (8%)
  other arithmetic  1.67 us (1%)
    pallas_call x1, Pallas kernels, local(): pl.pallas_call(functools.partial(kernel, tiles), out_shape=jax.ShapeDtype...  119 us
    broadcast_in_dim x1, local copies, waits for them, and re-layouts, local(): return jnp.transpose(result, (1, 0, 2))[None]  4.06 us
    unnamed x1, local copies, waits for them, and re-layouts  4.06 us

profile of v2, /device:TPU:0, one launch (start us, length us, event | category | flops | bytes accessed | tf_op | source)
XLA Modules:
  0.0 130.9 jit_solution(3503404335611510174)
XLA Ops:
  0.0 0.8 maximum_bitcast_fusion
  0.8 0.8 maximum_bitcast_fusion.1
  1.7 1.0 copy.10.ub
  2.7 1.0 copy.9.pb
  3.8 4.1 %copy.13 = bf16[1,64,8,2048]{3,1,2,0:T(8,128)(2,1)} copy(bf16[1,64,8,2048]{3,2,1,0:T(8,128)(2,1)} %param.5) | data formatting | bytes 4194304 | tf_op args[0]
  7.8 119.0 %shard_map.55 = bf16[8,64,2048]{2,1,0:T(8,128)(2,1)} custom-call(bf16[8,64,2048]{2,1,0:T(8,128)(2,1)} %bitcast.13, bf16[2,4,3,3,64,64]{5,4,3,2,1,0:T(8,128)(2,1)} %pw.1, bf16[2,4,3,3,64,64]{5,4,3,2,1,0:T(8,128)(2,1)} %uw.1, f32[2,4,128,1]{3,2,1,0:T(8,128)} %copy.9.pb, f32[2,4,128,1]{3,2,1,0:T(8,128)} %copy.10.ub), custom_call_target="tpu_custom_call" | custom-call | tf_op jit(solution)/shard_map/pallas_call | solution.py:377
  126.8 4.1 %copy.11 = bf16[1,64,8,2048]{3,2,1,0:T(8,128)(2,1)} copy(bf16[1,64,8,2048]{3,1,2,0:T(8,128)(2,1)} %bitcast.12) | data formatting | bytes 4194304 | tf_op jit(solution)/shard_map/broadcast_in_dim | solution.py:395

commit v3 on v2

--- a/solution.py
+++ b/solution.py
@@ -10,7 +10,7 @@
 LANES = 128
 MESSAGES = (
     "down0", "down1", "up0", "up1", "even0", "even1", "odd",
-    "hs0", "hs1", "hh0", "hh1", "x", "fs", "fh", "gs", "gh", "hl", "l1", "l2", "l3",
+    "hs0", "hs1", "hh0", "hh1", "x", "x2", "x3", "fs", "fh", "gs", "gh", "hl", "l1", "l2", "l3",
 )
 SLOT = {name: k for k, name in enumerate(MESSAGES)}
 LOCAL = ("own", "base", "keep", "out", "out2")
@@ -31,7 +31,7 @@
                     ]
 
 
-def kernel(tiles, own, pw, uw, pb, ub, out, e, h, b1, low, f2, h2, o2, l2, wa, wb, wc, wd, a_ref, c_ref, send_sem, recv_sem, local_sem):
+def kernel(tiles, own, pw, uw, pb, ub, out, e, h, b1, low, f2, h2, o2, l2, wa, wb, wc, wd, a_ref, c_ref, d_ref, send_sem, recv_sem, local_sem):
     own_rows, channels, width = own.shape
     half = own_rows // 2
     layers = pw.shape[1]
@@ -126,46 +126,58 @@
     build_weights(pw, 1, wc)
     build_weights(uw, 1, wd)
 
-    def network(src, base, dst, cols, keep, w_ref, b_ref, level, sign):
+    def network(src, base, dst, cols, keep, w_ref, b_ref, level, sign, await_halo):
         size = cols.stop - cols.start
         column = lax.broadcasted_iota(jnp.int32, (1, size), 1)
         first, final = column == 0, column == size - 1
-        rows = src.shape[0]
-        source = src
-        for layer in range(layers):
-            rows -= 2
-            last = layer == layers - 1
-            target = dst if last else (a_ref, c_ref)[layer % 2]
-
-            def pair(i, carry, source=source, target=target, layer=layer, last=last):
-                span = cols if layer == 0 else slice(0, size)
-                x = source[pl.ds(2 * i, 4), :, span].reshape(4 * channels, size)
-                acc = jnp.dot(w_ref[layer], x, preferred_element_type=jnp.float32)
-                group = 2 * channels
-                left = pltpu.roll(acc[:group], 1, 1)
-                right = pltpu.roll(acc[2 * group :], size - 1, 1)
-                y = (
-                    acc[group : 2 * group]
-                    + jnp.where(first, 0.0, left)
-                    + jnp.where(final, 0.0, right)
-                    + b_ref[level, layer]
-                )
-                for p in range(2):
-                    value = y[p * channels : (p + 1) * channels]
-                    if last:
-                        value = value[:, keep.start - cols.start : keep.stop - cols.start]
-                        old = base[2 * i + p, :, keep].astype(jnp.float32)
-                        value = old + value if sign > 0 else old - value
-                        target[2 * i + p, :, keep] = value.astype(jnp.bfloat16)
-                    else:
-                        g = first_row + layer + 1 + 2 * i + p
-                        inside = jnp.logical_and(g >= 0, g < tiles * own_rows)
-                        value = jnp.where(inside, jnp.maximum(value, 0.0), 0.0)
-                        target[2 * i + p, :, 0:size] = value.astype(jnp.bfloat16)
-                return carry
-
-            lax.fori_loop(0, rows // 2, pair, 0)
-            source = target
+        hidden = (a_ref, c_ref, d_ref)
+
+        def phase_step(phase, carry):
+            @pl.when(phase == 1)
+            def _():
+                await_halo()
+
+            source = src
+            for layer in range(layers):
+                count = (src.shape[0] - 2 * (layer + 1)) // 2
+                free = max(half - (layer + 1), 0)
+                last = layer == layers - 1
+                target = dst if last else hidden[layer]
+
+                def pair(i, carry, source=source, target=target, layer=layer, last=last):
+                    span = cols if layer == 0 else slice(0, size)
+                    x = source[pl.ds(2 * i, 4), :, span].reshape(4 * channels, size)
+                    acc = jnp.dot(w_ref[layer], x, preferred_element_type=jnp.float32)
+                    group = 2 * channels
+                    left = pltpu.roll(acc[:group], 1, 1)
+                    right = pltpu.roll(acc[2 * group :], size - 1, 1)
+                    y = (
+                        acc[group : 2 * group]
+                        + jnp.where(first, 0.0, left)
+                        + jnp.where(final, 0.0, right)
+                        + b_ref[level, layer]
+                    )
+                    for p in range(2):
+                        value = y[p * channels : (p + 1) * channels]
+                        if last:
+                            value = value[:, keep.start - cols.start : keep.stop - cols.start]
+                            old = base[2 * i + p, :, keep].astype(jnp.float32)
+                            value = old + value if sign > 0 else old - value
+                            target[2 * i + p, :, keep] = value.astype(jnp.bfloat16)
+                        else:
+                            g = first_row + layer + 1 + 2 * i + p
+                            inside = jnp.logical_and(g >= 0, g < tiles * own_rows)
+                            value = jnp.where(inside, jnp.maximum(value, 0.0), 0.0)
+                            target[2 * i + p, :, 0:size] = value.astype(jnp.bfloat16)
+                    return carry
+
+                begin = (1 - phase) * (1 - core) * (count - free) + phase * core * free
+                amount = (1 - phase) * free + phase * (count - free)
+                lax.fori_loop(begin, begin + amount, pair, 0)
+                source = target
+            return carry
+
+        lax.fori_loop(0, 2, phase_step, 0)
 
     def swap(name, field, cols):
         piece = field.at[mine, :, cols]
@@ -190,9 +202,7 @@
 
         swap(kind + "s" + k, field, cols).start()
 
-    def arrive(kind, k, field, cols):
-        swap_in(kind + "s" + k, field, cols).wait_recv()
-
+    def arrive_halo(kind, k, field, cols):
         @pl.when(has_halo)
         def _():
             halo_in(kind + "h" + k, field, cols).wait_recv()
@@ -212,41 +222,52 @@
                 own_copy.wait()
                 odd.wait_recv()
 
-            @pl.when(has_up)
-            def _():
-                downs(k).wait_recv()
-
         @pl.when(is_odd)
         def _():
             if k == 0:
                 base_copy.wait()
             evens(k).wait_recv()
 
-            @pl.when(has_down)
+        def frame_halo(k=k):
+            @pl.when(jnp.logical_and(is_even, has_up))
+            def _():
+                downs(k).wait_recv()
+
+            @pl.when(jnp.logical_and(is_odd, has_down))
             def _():
                 ups(k).wait_recv()
 
         reads = slice(0, block + LANES) if k == 0 else slice(part, width)
-        network(e, b1, h.at[mine], reads, hcut[k], wa, pb, 0, -1)
+        network(e, b1, h.at[mine], reads, hcut[k], wa, pb, 0, -1, frame_halo)
         share("h", str(k), h, hcut[k])
 
+    left, right = slice(0, block), slice(width - block, width)
+    near, far = slice(0, part), slice(part, width)
+    rest = slice(part, block)
+    tail = slice(block - part, block)
+    give_near = remote("x", low.at[:, :, near], f2.at[mine, :, near], across, t)
+    give_rest = remote("x2", low.at[:, :, rest], f2.at[mine, :, rest], across, t)
+    give_odd = remote("x3", low.at[:, :, right], o2, across, t)
+    keep_even = here("keep", low.at[:, :, right], f2.at[mine])
+    keep_odd = here("keep", low.at[:, :, left], o2)
     for k in range(2):
-        arrive("h", str(k), h, hcut[k])
+        swap_in("hs" + str(k), h, hcut[k]).wait_recv()
         reads = slice(0, block) if k == 0 else slice(width - block, width)
-        keep = slice(0, part) if k == 0 else slice(part, width)
-        network(h, e.at[mine], low, reads, keep, wb, ub, 0, 1)
+
+        def high_halo(k=k):
+            arrive_halo("h", str(k), h, hcut[k])
+
+        network(h, e.at[mine], low, reads, (near, far)[k], wb, ub, 0, 1, high_halo)
+
+        @pl.when(is_lower)
+        def _():
+            (give_near, give_rest)[k].start()
 
     high_out = here("out", h.at[: 2 * half], out)
-    left, right = slice(0, block), slice(width - block, width)
-    give_even = remote("x", low.at[:, :, right], f2.at[mine], across, t)
-    give_odd = remote("x", low.at[:, :, left], o2, across, t)
-    keep_even = here("keep", low.at[:, :, left], f2.at[mine])
-    keep_odd = here("keep", low.at[:, :, right], o2)
     every = slice(0, block)
 
     @pl.when(is_lower)
     def _():
-        give_even.start()
         keep_even.start()
         keep_even.wait()
 
@@ -254,7 +275,8 @@
     def _():
         give_odd.start()
         keep_odd.start()
-        give_even.wait_recv()
+        give_near.wait_recv()
+        give_rest.wait_recv()
 
     share("f", "", f2, every)
 
@@ -262,8 +284,6 @@
     def _():
         high_out.start()
 
-    arrive("f", "", f2, every)
-
     @pl.when(is_lower)
     def _():
         give_odd.wait_recv()
@@ -272,14 +292,13 @@
     def _():
         keep_odd.wait()
 
-    network(f2, o2, h2.at[mine], every, every, wc, pb, 1, -1)
+    swap_in("fs", f2, every).wait_recv()
+    network(f2, o2, h2.at[mine], every, every, wc, pb, 1, -1, lambda: arrive_halo("f", "", f2, every))
     share("g", "", h2, every)
-    arrive("g", "", h2, every)
-
-    near, far = slice(0, part), slice(part, width)
-    tail = slice(block - part, block)
-    high_send = remote("hl", h2.at[half:, :, near], out.at[:, :, near], across, t)
-    high_keep = here("out", h2.at[half:, :, tail], out.at[:, :, far])
+    swap_in("gs", h2, every).wait_recv()
+
+    high_send = remote("hl", h2.at[half:, :, tail], out.at[:, :, far], across, t)
+    high_keep = here("out", h2.at[half:, :, near], out.at[:, :, near])
     at_low = jnp.logical_and(is_even, is_lower)
     at_high = jnp.logical_and(is_even, is_upper)
 
@@ -291,12 +310,12 @@
     def _():
         high_keep.start()
 
-    network(h2, f2.at[mine], l2, every, every, wd, ub, 1, 1)
-
-    low_keep = here("out2", l2.at[:, :, near], out.at[:half, :, near])
-    first = remote("l1", l2.at[:, :, near], out.at[half:, :, near], partner, t)
-    second = remote("l2", l2.at[:, :, tail], out.at[:half, :, far], across, t)
-    third = remote("l3", l2.at[:, :, tail], out.at[half:, :, far], diagonal, t)
+    network(h2, f2.at[mine], l2, every, every, wd, ub, 1, 1, lambda: arrive_halo("g", "", h2, every))
+
+    low_keep = here("out2", l2.at[:, :, tail], out.at[:half, :, far])
+    first = remote("l1", l2.at[:, :, tail], out.at[half:, :, far], partner, t)
+    second = remote("l2", l2.at[:, :, near], out.at[:half, :, near], across, t)
+    third = remote("l3", l2.at[:, :, near], out.at[half:, :, near], diagonal, t)
 
     @pl.when(at_low)
     def _():
@@ -344,7 +363,8 @@
 
     @pl.when(is_lower)
     def _():
-        give_even.wait_send()
+        give_near.wait_send()
+        give_rest.wait_send()
 
     @pl.when(is_upper)
     def _():
@@ -384,6 +404,7 @@
             buffer(3 * half, block), buffer(3 * half, block), buffer(half, block), buffer(half, block),
             weight, weight, weight, weight,
             buffer(3 * half - 2, block + LANES), buffer(3 * half - 4, block + LANES),
+            buffer(3 * half - 6, block + LANES),
             pltpu.SemaphoreType.DMA((len(MESSAGES),)),
             pltpu.SemaphoreType.DMA((len(MESSAGES),)),
             pltpu.SemaphoreType.DMA((len(LOCAL),)),

time: 131 us -> 123 us (0.939)
  Pallas kernels: 119 us -> 110 us
    pallas_call x1, Pallas kernels: 119 us -> 110 us  [local(): pl.pallas_call(functools.partial(kernel, tiles), out_shape=jax.ShapeDtype...]
where the time goes in v3:
time: 123 us; the launch traced here: 122 us
  Pallas kernels  110 us (89%)
  local copies, waits for them, and re-layouts  10.2 us (8%)
  other arithmetic  1.67 us (1%)
    pallas_call x1, Pallas kernels, local(): pl.pallas_call(functools.partial(kernel, tiles), out_shape=jax.ShapeDtype...  110 us
    broadcast_in_dim x1, local copies, waits for them, and re-layouts, local(): return jnp.transpose(result, (1, 0, 2))[None]  4.06 us
    unnamed x1, local copies, waits for them, and re-layouts  4.06 us

profile of v3, /device:TPU:0, one launch (start us, length us, event | category | flops | bytes accessed | tf_op | source)
XLA Modules:
  0.0 122.4 jit_solution(12970255008505068588)
XLA Ops:
  0.0 0.8 maximum_bitcast_fusion
  0.8 0.8 maximum_bitcast_fusion.1
  1.7 1.0 copy.10.ub
  2.7 1.0 copy.9.pb
  3.8 4.1 %copy.13 = bf16[1,64,8,2048]{3,1,2,0:T(8,128)(2,1)} copy(bf16[1,64,8,2048]{3,2,1,0:T(8,128)(2,1)} %param.5) | data formatting | bytes 4194304 | tf_op args[0]
  7.8 110.5 %shard_map.55 = bf16[8,64,2048]{2,1,0:T(8,128)(2,1)} custom-call(bf16[8,64,2048]{2,1,0:T(8,128)(2,1)} %bitcast.13, bf16[2,4,3,3,64,64]{5,4,3,2,1,0:T(8,128)(2,1)} %pw.1, bf16[2,4,3,3,64,64]{5,4,3,2,1,0:T(8,128)(2,1)} %uw.1, f32[2,4,128,1]{3,2,1,0:T(8,128)} %copy.9.pb, f32[2,4,128,1]{3,2,1,0:T(8,128)} %copy.10.ub), custom_call_target="tpu_custom_call" | custom-call | tf_op jit(solution)/shard_map/pallas_call | solution.py:397
  118.3 4.1 %copy.11 = bf16[1,64,8,2048]{3,2,1,0:T(8,128)(2,1)} copy(bf16[1,64,8,2048]{3,1,2,0:T(8,128)(2,1)} %bitcast.12) | data formatting | bytes 4194304 | tf_op jit(solution)/shard_map/broadcast_in_dim | solution.py:416
